TPU v7x, 32 devices: a whole 2x2x4 slice. The times are simulated.
32 devices in a mesh: blk: 8 (over y, x, core), feat: 4 (over z).
Axes of the slice: x: 2, y: 2, z: 4, core: 2. Of those that a mesh axis runs over, the one named last changes fastest.
Arguments:
- features: bfloat16 [128, 8192], P('feat', 'blk'), may hold values from -6 to 6
- weight_in: bfloat16 [128, 256], replicated, may hold values from -0.5 to 0.5
- weight_mid: bfloat16 [256, 256], replicated, may hold values from -0.375 to 0.375
- weight_out: bfloat16 [256, 172], replicated, may hold values from -0.375 to 0.375
- block_values: bfloat16 [8, 8, 16, 128, 128], P('blk'), may hold values from -0.25 to 0.25
- block_dst: int32 [8, 8, 16], P('blk'), may hold values from 0 to 7
- block_src: int32 [8, 8, 16], P('blk'), may hold values from 0 to 7
- block_count: int32 [8, 8], P('blk'), may hold values from 4 to 16, as said below
- labels: int32 [8192], P('blk'), may hold values from 0 to 171
- train_mask: int32 [8192], P('blk'), may hold values from 0 to 1
Outputs:
- loss: float32 [], replicated
- grad_in: float32 [128, 256], P('feat')
- grad_mid: float32 [256, 256], P('feat')
- grad_out: float32 [256, 172], P('feat')
Inputs may be any that keep to these rules, and one draw needn't show every extreme that they name: block_count[b, p] is the number of live slots of the blocks of panel b's rows that read panel p's nodes; block_count[b, b] = 16. Entries of block_dst, block_src and block_values at slots at or past block_count are unused.
All inputs are finite; a program needn't handle non-finite values.
Results may differ from a plain program's by a relative error of at most 0.017.
Values may be sent and summed in bfloat16 or wider, within the bound.
A program may use at most 64 MiB of HBM per device.

v0:
```python
import jax
import jax.numpy as jnp
from jax import lax
from jax.sharding import PartitionSpec as P


def elu(values):
    return jnp.where(values > 0, values, jnp.expm1(values))


def elu_slope(values):
    return jnp.where(values > 0, 1.0, jnp.exp(values))


def panel_folder(values, targets, sources, live_count, breadth, row_blocks, block_size):
    panel_rows = row_blocks * block_size
    slot_index = jnp.arange(values.shape[2], dtype=jnp.int32)

    def folding(running, portion, offset):
        several = portion.shape[1] // panel_rows

        def folding_one_panel(turn_index, accumulated):
            window = lax.dynamic_slice_in_dim(portion, turn_index * panel_rows, panel_rows, 1)
            window = window.reshape(breadth, row_blocks, block_size)
            chosen = jnp.take(window, sources[0, turn_index], axis=1)
            product = jnp.einsum(
                "fsj,sij->fsi", chosen, values[0, turn_index], preferred_element_type=jnp.float32
            )
            live_slots = (slot_index < live_count[0, turn_index]).astype(jnp.float32)
            return accumulated.at[:, targets[0, turn_index]].add(
                product * live_slots[None, :, None]
            )

        return lax.fori_loop(0, several, folding_one_panel, running)

    return folding


def hidden_aggregate(table, values, targets, sources, live_count):
    breadth, panel_rows = table.shape
    block_size = values.shape[-1]
    row_blocks = panel_rows // block_size
    folding = panel_folder(values, targets, sources, live_count, breadth, row_blocks, block_size)
    initial = jnp.zeros((breadth, row_blocks, block_size), jnp.float32)
    summed = folding(initial, lax.all_gather(table, "blk", axis=1, tiled=True), jnp.int32(0))
    return summed.reshape(breadth, panel_rows).astype(jnp.bfloat16)


def spread_back(grads, values, targets, sources, live_count):
    breadth, panel_rows = grads.shape
    block_size = values.shape[-1]
    row_blocks = panel_rows // block_size
    tiles = grads.reshape(breadth, row_blocks, block_size)
    slot_index = jnp.arange(values.shape[2], dtype=jnp.int32)

    def term_one_panel(source_panel):
        chosen = jnp.take(tiles, targets[0, source_panel], axis=1)
        product = jnp.einsum(
            "fsi,sij->fsj", chosen, values[0, source_panel], preferred_element_type=jnp.float32
        )
        live_slots = (slot_index < live_count[0, source_panel]).astype(jnp.float32)
        placed = jnp.zeros((breadth, row_blocks, block_size), jnp.float32)
        placed = placed.at[:, sources[0, source_panel]].add(product * live_slots[None, :, None])
        return placed.reshape(breadth, panel_rows)

    summed = lax.psum_scatter(
        lax.map(term_one_panel, jnp.arange(lax.axis_size("blk") * 1, dtype=jnp.int32)).astype(
            jnp.bfloat16
        ),
        "blk",
        scatter_dimension=0,
        tiled=True,
    ).astype(jnp.float32)
    return summed[0]


def mix_features(weight, table):
    out_part = weight.shape[1] // lax.axis_size("feat")
    position = lax.axis_index("feat")
    own_columns = lax.dynamic_slice_in_dim(weight, position * out_part, out_part, 1)
    return lax.dot_general(
        own_columns,
        lax.all_gather(table, "feat", axis=0, tiled=True),
        (((0,), (0,)), ((), ())),
        preferred_element_type=jnp.float32,
    )


def class_scores(weight_out, table):
    return lax.dot_general(
        weight_out,
        lax.all_gather(table, "feat", axis=0, tiled=True),
        (((0,), (0,)), ((), ())),
        preferred_element_type=jnp.float32,
    )


def weight_columns(gated, own_table, own_weight):
    breadth, panel_rows = own_table.shape
    total_out = gated.shape[0] * lax.axis_size("feat")

    def add_columns(running, portion):
        grad_part = running[0]
        product = lax.dot_general(
            own_table, portion, (((1,), (1,)), ((), ())), preferred_element_type=jnp.float32
        )
        grad_part = product
        if len(running) == 1:
            return (grad_part,)
        return (grad_part, jnp.dot(own_weight, portion, preferred_element_type=jnp.float32))

    grad_zero = jnp.zeros((breadth, total_out), jnp.float32)
    if own_weight is None:
        initial = (grad_zero,)
    else:
        initial = (grad_zero, jnp.zeros((own_weight.shape[0], panel_rows), jnp.float32))
    return add_columns(initial, lax.all_gather(gated, "feat", axis=0, tiled=True))


def shards(
    features,
    weight_in,
    weight_mid,
    weight_out,
    block_values,
    block_dst,
    block_src,
    block_count,
    labels,
    train_mask,
):
    position = lax.axis_index("feat")
    hidden_part = weight_mid.shape[0] // lax.axis_size("feat")
    block_size = block_values.shape[-1]
    in_part, panel_rows = features.shape
    row_blocks = panel_rows // block_size
    folding = panel_folder(
        block_values, block_dst, block_src, block_count, in_part, row_blocks, block_size
    )
    initial = jnp.zeros((in_part, row_blocks, block_size), jnp.float32)
    first_sum = folding(initial, lax.all_gather(features, "blk", axis=1, tiled=True), jnp.int32(0))
    first_agg = first_sum.reshape(in_part, panel_rows).astype(jnp.bfloat16)
    first_pre = mix_features(weight_in, first_agg)
    first_act = elu(first_pre).astype(jnp.bfloat16)
    second_agg = hidden_aggregate(first_act, block_values, block_dst, block_src, block_count)
    second_pre = mix_features(weight_mid, second_agg)
    second_act = elu(second_pre).astype(jnp.bfloat16)
    third_agg = hidden_aggregate(second_act, block_values, block_dst, block_src, block_count)
    out_rows = lax.dynamic_slice_in_dim(weight_out, position * hidden_part, hidden_part, 0)
    logits = class_scores(weight_out, third_agg)
    log_total = jnp.log(jnp.sum(jnp.exp(logits), axis=0))
    one_hot = (jnp.arange(logits.shape[0], dtype=jnp.int32)[:, None] == labels[None, :]).astype(
        jnp.float32
    )
    picked = jnp.sum(one_hot * logits, axis=0)
    weighting = train_mask.astype(jnp.float32)
    loss_total, node_count = lax.psum(
        (jnp.sum(weighting * (log_total - picked)), jnp.sum(weighting)), "blk"
    )
    loss = loss_total / jnp.maximum(node_count, 1.0)
    grad_logits = (weighting[None, :] * (jnp.exp(logits - log_total[None, :]) - one_hot)).astype(
        jnp.bfloat16
    )
    grad_out = lax.dot_general(
        third_agg, grad_logits, (((1,), (1,)), ((), ())), preferred_element_type=jnp.float32
    )
    grad_out = lax.psum(grad_out, "blk")
    third_back = jnp.dot(out_rows, grad_logits, preferred_element_type=jnp.float32).astype(
        jnp.bfloat16
    )
    second_grad = spread_back(third_back, block_values, block_dst, block_src, block_count)
    second_gate = (second_grad * elu_slope(second_pre)).astype(jnp.bfloat16)
    mid_rows = lax.dynamic_slice_in_dim(weight_mid, position * hidden_part, hidden_part, 0)
    grad_mid, second_back = weight_columns(second_gate, second_agg, mid_rows)
    grad_mid = lax.psum(grad_mid, "blk")
    first_grad = spread_back(
        second_back.astype(jnp.bfloat16), block_values, block_dst, block_src, block_count
    )
    first_gate = (first_grad * elu_slope(first_pre)).astype(jnp.bfloat16)
    grad_in = weight_columns(first_gate, first_agg, None)[0]
    grad_in = lax.psum(grad_in, "blk")
    grad_in, grad_mid, grad_out = (grad_in, grad_mid, grad_out)
    return (loss, grad_in, grad_mid, grad_out)


def solution(mesh):
    placed = (
        P("feat", "blk"),
        P(),
        P(),
        P(),
        P("blk", None, None, None, None),
        P("blk", None, None),
        P("blk", None, None),
        P("blk", None),
        P("blk"),
        P("blk"),
    )
    return jax.shard_map(
        shards,
        mesh=mesh,
        in_specs=placed,
        out_specs=(P(), P("feat", None), P("feat", None), P("feat", None)),
        check_vma=False,
    )
```

profile of v0, /device:TPU:0, one launch (start us, length us, event | category | flops | bytes accessed | tf_op | source)
XLA Modules:
  0.0 608.6 jit_solution(1737324306972229232)
XLA Ops:
  7.2 11.6 %all_gather.24 = bf16[32,8192]{1,0:T(8,128)(2,1)S(1)} all-gather(bf16[32,1024]{1,0:T(8,128)(2,1)} %param.22), channel_id=1, replica_groups=mesh['blk'=8,'feat'=4] {'blk'}, dimensions={1}, use_global_device_ids=true | all-gather | bytes 589824 | tf_op jit(solution)/shard_map/all_gather | solution.py:141
  18.9 53.0 %while.64 = (s32[]{:T(128)}, f32[32,8,128]{2,0,1:T(8,128)S(1)}, s32[1,8,16]{2,1,0:T(8,128)}, bf16[1,8,16,128,128]{4,3,2,1,0:T(8,128)(2,1)}, s32[1,8,16]{2,1,0:T(...) while((s32[]{:T(128)}, f32[32,8,128]{2,0,1:T(8,128)S(1)}, ...), condition=%wide.region_2.3_spmd.clone, body=%wide.region_0.2_spmd.clone.sunk | while | flops 16975076 | bytes 2102115 | solution.py:34
  22.8 1.5 fusion.121
  29.4 1.5 fusion.121
  36.1 1.5 fusion.121
  42.7 1.5 fusion.121
  49.3 1.5 fusion.121
  55.9 1.5 fusion.121
  71.9 14.1 %all_gather.25 = bf16[128,1024]{1,0:T(8,128)(2,1)S(1)} all-gather(bf16[32,1024]{1,0:T(8,128)(2,1)S(1)} %copy_bitcast_fusion.7), channel_id=1, replica_groups=mesh['blk'=8,'feat'=4] {'feat'}, dimensions={0}, use_global_device_ids=true | all-gather | bytes 327680 | tf_op jit(solution)/shard_map/all_gather | solution.py:83
  87.1 24.1 %all-gather.3.cloned.1.call-done = bf16[64,8192]{1,0:T(8,128)(2,1)} async-done(((bf16[64,1024]{1,0:T(8,128)(2,1)}), bf16[64,8192]{1,0:T(8,128)(2,1)}) %all-gather.3.cloned.1.call-update) | async-done | bytes 1048592 | tf_op jit(solution)/shard_map/all_gather | solution.py:45
  111.2 62.0 %while.65 = (s32[]{:T(128)}, f32[64,8,128]{2,0,1:T(8,128)S(1)}, s32[1,8,16]{2,1,0:T(8,128)}, bf16[1,8,16,128,128]{4,3,2,1,0:T(8,128)(2,1)}, bf16[64,8192]{1,0:T(...) while((s32[]{:T(128)}, f32[64,8,128]{2,0,1:T(8,128)S(1)}, ...), condition=%wide.region_5.7_spmd.clone, body=%wide.region_3.0_spmd.clone.sunk | while | flops 33948852 | bytes 3674915 | solution.py:34
  116.1 1.5 fusion.125
  123.8 1.5 fusion.125
  131.6 1.5 fusion.125
  139.3 1.5 fusion.125
  147.1 1.5 fusion.125
  154.8 1.5 fusion.125
  162.6 1.5 fusion.125
  170.3 1.5 fusion.125
  173.3 16.0 %all_gather.27 = bf16[256,1024]{1,0:T(8,128)(2,1)S(1)} all-gather(bf16[64,1024]{1,0:T(8,128)(2,1)S(1)} %copy_bitcast_fusion.4), channel_id=1, replica_groups=mesh['blk'=8,'feat'=4] {'feat'}, dimensions={0}, use_global_device_ids=true | all-gather | bytes 655360 | tf_op jit(solution)/shard_map/all_gather | solution.py:83
  190.4 23.9 %all-gather.5.cloned.1.call-done = bf16[64,8192]{1,0:T(8,128)(2,1)} async-done(((bf16[64,1024]{1,0:T(8,128)(2,1)}), bf16[64,8192]{1,0:T(8,128)(2,1)}) %all-gather.5.cloned.1.call-update) | async-done | bytes 1048592 | tf_op jit(solution)/shard_map/all_gather | solution.py:45
  214.4 62.0 %while.66 = (s32[]{:T(128)}, f32[64,8,128]{2,0,1:T(8,128)S(1)}, s32[1,8,16]{2,1,0:T(8,128)}, bf16[1,8,16,128,128]{4,3,2,1,0:T(8,128)(2,1)}, bf16[64,8192]{1,0:T(...) while((s32[]{:T(128)}, f32[64,8,128]{2,0,1:T(8,128)S(1)}, ...), condition=%wide.region_8.10_spmd.clone, body=%wide.region_6.9_spmd.clone.sunk | while | flops 33948852 | bytes 3674915 | solution.py:34
  219.2 1.5 fusion.129
  227.0 1.5 fusion.129
  234.7 1.5 fusion.129
  242.5 1.5 fusion.129
  250.2 1.5 fusion.129
  258.0 1.5 fusion.129
  265.7 1.5 fusion.129
  273.5 1.5 fusion.129
  276.4 16.0 %all_gather.29 = bf16[256,1024]{1,0:T(8,128)(2,1)S(1)} all-gather(bf16[64,1024]{1,0:T(8,128)(2,1)S(1)} %copy_bitcast_fusion.3), channel_id=1, replica_groups=mesh['blk'=8,'feat'=4] {'feat'}, dimensions={0}, use_global_device_ids=true | all-gather | bytes 655360 | tf_op jit(solution)/shard_map/all_gather | solution.py:92
  294.1 75.6 %while.67 = (s32[]{:T(128)}, bf16[8,64,1024]{2,1,0:T(8,128)(2,1)S(1)}, s32[8]{0:T(128)S(1)}, s32[1,8,16]{2,1,0:T(8,128)}, bf16[1,8,16,128,128]{4,3,2,1,0:T(8,128...) while((s32[]{:T(128)}, ...), condition=%wide.region_17.19_spmd.clone, body=%wide.region_15.18_spmd.clone.sunk | while | flops 33948852 | bytes 4592431 | solution.py:67
  370.7 36.5 %reduce-scatter.3.cloned.1.call-done = bf16[1,64,1024]{2,1,0:T(8,128)(2,1)} async-done(((bf16[8,64,1024]{2,1,0:T(8,128)(2,1)}), bf16[1,64,1024]{2,1,0:T(8,128)(2,1)}) %reduce-scatter.3.cloned.1.call-update) | async-done | bytes 131088 | tf_op jit(solution)/shard_map/reduce_scatter | solution.py:66
  408.2 15.4 %all_gather.30 = bf16[256,1024]{1,0:T(8,128)(2,1)S(1)} all-gather(bf16[64,1024]{1,0:T(8,128)(2,1)S(1)} %fusion.75), channel_id=1, replica_groups=mesh['blk'=8,'feat'=4] {'feat'}, dimensions={0}, use_global_device_ids=true | all-gather | bytes 655360 | tf_op jit(solution)/shard_map/all_gather | solution.py:117
  424.0 80.9 %while.68 = (s32[]{:T(128)}, bf16[8,64,1024]{2,1,0:T(8,128)(2,1)S(1)}, s32[8]{0:T(128)S(1)}, s32[1,8,16]{2,1,0:T(8,128)}, bf16[1,8,16,128,128]{4,3,2,1,0:T(8,128...) while((s32[]{:T(128)}, ...), condition=%wide.region_21.23_spmd.clone, body=%wide.region_19.22_spmd.clone.sunk | while | flops 33948852 | bytes 4592743 | solution.py:67
  432.3 1.5 scatter_fusion.4
  442.5 1.5 scatter_fusion.4
  452.6 1.5 scatter_fusion.4
  462.7 1.5 scatter_fusion.4
  472.8 1.5 scatter_fusion.4
  482.9 1.5 scatter_fusion.4
  493.0 1.5 scatter_fusion.4
  503.1 1.5 scatter_fusion.4
  508.3 34.5 %reduce-scatter.5.cloned.1.call-done = bf16[1,64,1024]{2,1,0:T(8,128)(2,1)} async-done(((bf16[8,64,1024]{2,1,0:T(8,128)(2,1)}), bf16[1,64,1024]{2,1,0:T(8,128)(2,1)}) %reduce-scatter.5.cloned.1.call-update) | async-done | bytes 131088 | tf_op jit(solution)/shard_map/reduce_scatter | solution.py:66
  543.7 15.4 %all_gather.31 = bf16[256,1024]{1,0:T(8,128)(2,1)S(1)} all-gather(bf16[64,1024]{1,0:T(8,128)(2,1)S(1)} %fusion.73), channel_id=1, replica_groups=mesh['blk'=8,'feat'=4] {'feat'}, dimensions={0}, use_global_device_ids=true | all-gather | bytes 655360 | tf_op jit(solution)/shard_map/all_gather | solution.py:117
  559.4 24.2 %all-reduce.5 = (f32[]{:T(128)}, f32[]{:T(128)}, f32[32,256]{1,0:T(8,128)}, f32[64,172]{1,0:T(8,128)}) all-reduce(f32[]{:T(128)} %get-tuple-element.640, f32[]{:T(128)} %get-tuple-element.639, f32[32,256]{1,0:T(8,128)S(1)} %fusion.88, f32[64,172]{1,0:T(8,128)S(1)} %fusion.90), channel_id=1, replica_groups=mesh['blk'=8,'feat'=4] {'blk'}, use_global_device_ids=true, to_apply=%region_12.14 | all-reduce | flops 19202 | bytes 153616 | tf_op jit(solution)/shard_map/psum | solution.py:157
  584.8 14.6 %all-reduce.4.cloned.1.call-done = f32[64,256]{1,0:T(8,128)} async-done(((f32[64,256]{1,0:T(8,128)}), f32[64,256]{1,0:T(8,128)}) %all-reduce.4.cloned.1.call-update) | async-done | bytes 65552 | tf_op jit(solution)/shard_map/psum | solution.py:175
  599.5 1.5 copy.108
  (436 shorter events, 265.5 us)
Async XLA Ops:
  7.2 182.1 %copy-start = (bf16[256,256]{1,0:T(8,128)(2,1)S(1)}, bf16[256,256]{1,0:T(8,128)(2,1)}, u32[]{:S(2)}) copy-start(bf16[256,256]{1,0:T(8,128)(2,1)} %param.24) | copy-start | bytes 393220
  7.2 104.0 %all-gather.3.cloned.1.call-start = ((), (), s32[]{:S(2)}) async-start(), calls=%async_computation.2 | async-start | bytes 1179648 | tf_op jit(solution)/shard_map/all_gather | solution.py:45
  18.9 67.1 %copy-start.6 = (bf16[128,256]{1,0:T(8,128)(2,1)S(1)}, bf16[128,256]{1,0:T(8,128)(2,1)}, u32[]{:S(2)}) copy-start(bf16[128,256]{1,0:T(8,128)(2,1)} %param.23) | copy-start | bytes 196612
  87.0 127.3 %all-gather.5.cloned.1.call-start = ((), (), s32[]{:S(2)}) async-start(), calls=%async_computation.3 | async-start | bytes 1179648 | tf_op jit(solution)/shard_map/all_gather | solution.py:45
  111.2 79.1 %copy-start.7 = (s32[1024]{0:T(1024)S(1)}, s32[1024]{0:T(1024)}, u32[]{:S(2)}) copy-start(s32[1024]{0:T(1024)} %param.31) | copy-start | bytes 12292
  190.3 216.9 %reduce-scatter.3.cloned.1.call-start = ((), (), s32[]{:S(2)}) async-start(), calls=%async_computation.4 | async-start | bytes 1179648 | tf_op jit(solution)/shard_map/reduce_scatter | solution.py:66
  214.3 78.1 %copy-start.4 = (bf16[256,172]{0,1:T(8,128)(2,1)S(1)}, bf16[256,172]{0,1:T(8,128)(2,1)}, u32[]{:S(2)}) copy-start(bf16[256,172]{0,1:T(8,128)(2,1)} %param.25) | copy-start | bytes 264196
  214.3 78.1 %copy-start.5 = (s32[1024]{0:T(1024)S(1)}, s32[1024]{0:T(1024)}, u32[]{:S(2)}) copy-start(s32[1024]{0:T(1024)} %param.30) | copy-start | bytes 12292
  292.7 1.2 copy-start.3
  369.7 1.0 copy-start.1
  370.7 172.1 %reduce-scatter.5.cloned.1.call-start = ((), (), s32[]{:S(2)}) async-start(), calls=%async_computation.5 | async-start | bytes 1179648 | tf_op jit(solution)/shard_map/reduce_scatter | solution.py:66
  424.0 3.8 copy-start.8
  432.3 1.8 copy-start.9
  434.1 3.8 copy-start.8
  442.4 1.8 copy-start.9
  444.2 3.8 copy-start.8
  452.5 1.8 copy-start.9
  454.3 3.8 copy-start.8
  462.6 1.8 copy-start.9
  464.4 3.8 copy-start.8
  472.7 1.8 copy-start.9
  474.5 3.8 copy-start.8
  482.9 1.8 copy-start.9
  484.7 3.8 copy-start.8
  493.0 1.8 copy-start.9
  494.8 3.8 copy-start.8
  503.1 1.8 copy-start.9
  504.9 1.0 copy-start.2
  505.9 93.6 %all-reduce.4.cloned.1.call-start = ((), (), s32[]{:S(2)}) async-start(), calls=%async_computation.6 | async-start | bytes 131072 | tf_op jit(solution)/shard_map/psum | solution.py:175
Sparse Core Ops, SparseCore 0:
  87.1 24.0 all-gather.2
  190.4 23.8 all-gather.4
  370.8 36.3 reduce-scatter.2
  506.0 36.7 reduce-scatter.4
  546.2 53.1 all-reduce.3
where the time goes:
time: 615 us; the launch traced here: 609 us
  other arithmetic  142 us (23%)
  waiting for transfers between devices  134 us (22%)
  blocking collectives  113 us (18%)
  local copies, waits for them, and re-layouts  106 us (17%)
  matrix products  63.7 us (10%)
  loops' own time  33.6 us (5%)
  between operations  16.4 us (3%)
    reduce_scatter x2, waiting for transfers between devices, spread_back(): lax.psum_scatter(lax.map(term_one_panel, jnp.arange(lax.axis_size('blk')...  71 us
    all_gather x2, waiting for transfers between devices, hidden_aggregate(): lax.all_gather(table, 'blk', axis=1, tiled=True)  48.1 us
    dot_general x24, matrix products, folding_one_panel(): jnp.einsum('fsj,sij->fsi', chosen, values[0, turn_index], preferred_eleme...  36.4 us
    another operation x2, loops' own time, spread_back(): lax.map(term_one_panel, jnp.arange(lax.axis_size('blk') * 1, dtype=jnp.in...  32.5 us
    scatter-add x24, other arithmetic, folding_one_panel(): accumulated.at[:, targets[0, turn_index]]  31.2 us
    all_gather x2, blocking collectives, weight_columns(): lax.all_gather(gated, 'feat', axis=0, tiled=True)  30.8 us
    all_gather x2, blocking collectives, mix_features(): lax.all_gather(table, 'feat', axis=0, tiled=True)  30.1 us
    dynamic_slice x24, local copies, waits for them, and re-layouts, folding_one_panel(): live_slots = (slot_index < live_count[0, turn_index]).astype(jnp.float32)  29.8 us
  transfers between devices with their start and end apart: 5, of which 5 were waited for; matrix products, arithmetic and copies ran while one was open for 1% of the time, Pallas kernels for 0%

commit v1 on v0

v1 whole, which is shorter than its diff:
```python
import functools

import jax
import jax.numpy as jnp
from jax import lax
from jax.experimental import pallas as pl
from jax.experimental.pallas import tpu as pltpu
from jax.sharding import PartitionSpec as P

MESH = pl.DeviceIdType.MESH
NT = (((1,), (1,)), ((), ()))
F32 = jnp.float32
BF16 = jnp.bfloat16


def dot(a, b):
    return jnp.dot(a, b, preferred_element_type=F32)


def dot_nt(a, b):
    return lax.dot_general(a, b, NT, preferred_element_type=F32)


def elu(v):
    return jnp.where(v > 0, v, jnp.exp(jnp.minimum(v, 0.0)) - 1.0)


def elu_slope(v):
    return jnp.where(v > 0, 1.0, jnp.exp(jnp.minimum(v, 0.0)))


class Line:
    def __init__(self, table, sems, nf):
        self.table, self.sems, self.nf = table, sems, nf
        self.f = lax.axis_index("feat")

    def right(self, k):
        return pltpu.make_async_remote_copy(
            src_ref=self.table.at[self.f - k],
            dst_ref=self.table.at[self.f - k],
            send_sem=self.sems.at[0, k],
            recv_sem=self.sems.at[1, k + 1],
            device_id={"feat": self.f + 1},
            device_id_type=MESH,
        )

    def left(self, k):
        return pltpu.make_async_remote_copy(
            src_ref=self.table.at[self.f + k],
            dst_ref=self.table.at[self.f + k],
            send_sem=self.sems.at[2, k],
            recv_sem=self.sems.at[3, k + 1],
            device_id={"feat": self.f - 1},
            device_id_type=MESH,
        )

    def arrived(self, sem, slot):
        pltpu.make_async_copy(self.table.at[slot], self.table.at[slot], sem).wait()

    def start(self):
        @pl.when(self.f < self.nf - 1)
        def _():
            self.right(0).start()

        @pl.when(self.f > 0)
        def _():
            self.left(0).start()

    def finish(self):
        f, nf = self.f, self.nf
        for k in range(1, nf):

            @pl.when(f >= k)
            def _():
                self.arrived(self.sems.at[1, k], f - k)

                @pl.when(f < nf - 1)
                def _():
                    self.right(k).start()

            @pl.when(f + k <= nf - 1)
            def _():
                self.arrived(self.sems.at[3, k], f + k)

                @pl.when(f > 0)
                def _():
                    self.left(k).start()

        for k in range(nf):

            @pl.when(jnp.logical_and(f >= k, f < nf - 1))
            def _():
                self.right(k).wait_send()

            @pl.when(jnp.logical_and(f + k <= nf - 1, f > 0))
            def _():
                self.left(k).wait_send()


def step_kernel(
    n, nf, classes, slots,
    features, w_in, w_mid, w_out, out_rows, mid_rows, values,
    dst, src, w_fwd, w_bwd, labels, mask,
    loss_out, gin_out, gmid_out, gout_out,
    tab1, tab2, tab3, line1, line2, line3, line4, line5,
    back, acc, prod, win1, acc1, prod1, pre1, pre2,
    out_p, recv_p, out_s, recv_s,
    go_mine, go_part, go_pair, go_recv,
    gm_mine, gm_part, gm_pair, gm_recv,
    gi_mine, gi_part, gi_pair, gi_recv,
    blk_sems, line_sems, rs_sems, sum_sems,
):
    me = lax.axis_index("blk")
    f = lax.axis_index("feat")
    chip = me // 2
    side = me % 2
    chips = n // 2
    partner = chip * 2 + (1 - side)
    rb_count = tab2.shape[1]
    blk = tab2.shape[3]

    def far(k):
        return lax.rem(chip + k, chips) * 2 + side

    barrier = pltpu.get_barrier_semaphore()
    pl.semaphore_signal(barrier, inc=1, device_id={"blk": partner}, device_id_type=MESH)
    for k in range(1, chips):
        pl.semaphore_signal(barrier, inc=1, device_id={"blk": far(k)}, device_id_type=MESH)
    for other in (lax.rem(f + 1, nf), lax.rem(f + nf - 1, nf)):
        pl.semaphore_signal(barrier, inc=1, device_id={"feat": other}, device_id_type=MESH)
    pl.semaphore_wait(barrier, chips + 2)

    def remote(source, target, send, recv, device):
        return pltpu.make_async_remote_copy(
            src_ref=source, dst_ref=target, send_sem=send, recv_sem=recv,
            device_id={"blk": device}, device_id_type=MESH,
        )

    def lanes(rb):
        return slice(rb * blk, (rb + 1) * blk)

    def combine(product, weights, panel, rb):
        total = None
        for s in range(slots):
            term = product[s] * weights[(panel * slots + s) * rb_count + rb]
            total = term if total is None else total + term
        return total

    def aggregate(table, phase, total, product, window):
        def to_far(k):
            return remote(table.at[me], table.at[me], blk_sems.at[phase, 0, k],
                          blk_sems.at[phase, 1, k], far(k))

        def to_partner(k):
            panel = lax.rem(chip - k + chips, chips) * 2 + side
            return remote(table.at[panel], table.at[panel], blk_sems.at[phase, 2, k],
                          blk_sems.at[phase, 3, k], partner)

        for k in range(1, chips):
            to_far(k).start()
        to_partner(0).start()
        total[...] = jnp.zeros_like(total)

        def turn(t, carry):
            k = t // 2
            h = t % 2
            base = lax.rem(chip - k + chips, chips) * 2

            @pl.when(jnp.logical_and(h == 0, k > 0))
            def _():
                to_far(k).wait_recv()
                to_partner(k).start()

            @pl.when(h == 1)
            def _():
                to_partner(k).wait_recv()

            panel = base + jnp.where(h == 0, side, 1 - side)
            window[...] = table[panel]
            for s in range(slots):
                chosen = window[src[panel * slots + s]]
                product[s] = dot_nt(chosen, values[panel, s])
            for rb in range(rb_count):
                total[rb] += combine(product, w_fwd, panel, rb)
            return carry

        lax.fori_loop(0, n, turn, 0)
        for k in range(1, chips):
            to_far(k).wait_send()
        for k in range(chips):
            to_partner(k).wait_send()

    def spread(phase, own):
        def to_partner(k):
            return remote(out_p.at[phase, k], recv_p.at[phase, k], rs_sems.at[phase, 0, k],
                          rs_sems.at[phase, 1, k], partner)

        def to_far(k):
            return remote(out_s.at[phase, k], recv_s.at[phase, k], rs_sems.at[phase, 2, k],
                          rs_sems.at[phase, 3, k], far(k))

        def turn(t, carry):
            k = lax.rem(t // 2 + 1, chips)
            h = t % 2
            panel = lax.rem(chip + k, chips) * 2 + jnp.where(h == 0, 1 - side, side)
            for s in range(slots):
                chosen = back[dst[panel * slots + s]]
                prod[s] = dot(chosen, values[panel, s])
            for rb in range(rb_count):
                own[rb] = combine(prod, w_bwd, panel, rb)

            @pl.when(h == 0)
            def _():
                out_p[phase, k] = own[...].astype(BF16)
                to_partner(k).start()

            @pl.when(h == 1)
            def _():
                to_partner(k).wait_recv()
                own[...] += recv_p[phase, k].astype(F32)

                @pl.when(k > 0)
                def _():
                    out_s[phase, k] = own[...].astype(BF16)
                    to_far(k).start()

            return carry

        lax.fori_loop(0, n, turn, 0)
        for k in range(1, chips):
            to_far(k).wait_recv()
            own[...] += recv_s[phase, k].astype(F32)
        for k in range(1, chips):
            to_far(k).wait_send()
        for k in range(chips):
            to_partner(k).wait_send()

    class Total:
        def __init__(self, index, mine, part, pair, recv):
            self.index, self.mine, self.part, self.pair, self.recv = index, mine, part, pair, recv

        def near(self):
            return remote(self.mine, self.part, sum_sems.at[self.index, 0, 0],
                          sum_sems.at[self.index, 1, 0], partner)

        def wide(self, k):
            return remote(self.pair, self.recv.at[chip], sum_sems.at[self.index, 0, k],
                          sum_sems.at[self.index, 1, k], far(k))

        def spread_pair(self):
            self.near().wait_recv()
            self.pair[...] = self.mine[...] + self.part[...]
            for k in range(1, chips):
                self.wide(k).start()

        def result(self):
            self.recv[chip] = self.pair[...]
            for k in range(1, chips):
                source = lax.rem(chip - k + chips, chips)
                remote(self.pair, self.recv.at[source], sum_sems.at[self.index, 0, k],
                       sum_sems.at[self.index, 1, k], far(k)).wait_recv()
            total = self.recv[0]
            for c in range(1, chips):
                total = total + self.recv[c]
            self.near().wait_send()
            for k in range(1, chips):
                self.wide(k).wait_send()
            return total

    for rb in range(rb_count):
        tab1[me, rb] = features[:, lanes(rb)]
    aggregate(tab1, 0, acc1, prod1, win1)
    for rb in range(rb_count):
        line1[f, :, lanes(rb)] = acc1[rb].astype(BF16)
    gather = Line(line1, line_sems.at[0], nf)
    gather.start()
    gather.finish()
    pre = dot(w_in[0], line1[0])
    for g in range(1, nf):
        pre += dot(w_in[g], line1[g])
    pre1[...] = pre
    act = elu(pre).astype(BF16)
    for rb in range(rb_count):
        tab2[me, rb] = act[:, lanes(rb)]

    aggregate(tab2, 1, acc, prod, back)
    for rb in range(rb_count):
        line2[f, :, lanes(rb)] = acc[rb].astype(BF16)
    gather = Line(line2, line_sems.at[1], nf)
    gather.start()
    gather.finish()
    hidden = nf * line2.shape[1]
    nodes = line2.shape[2]
    pre = dot(w_mid[...], line2[...].reshape(hidden, nodes))
    pre2[...] = pre
    act = elu(pre).astype(BF16)
    for rb in range(rb_count):
        tab3[me, rb] = act[:, lanes(rb)]

    aggregate(tab3, 2, acc, prod, back)
    for rb in range(rb_count):
        line3[f, :, lanes(rb)] = acc[rb].astype(BF16)
    gather = Line(line3, line_sems.at[2], nf)
    gather.start()
    gather.finish()
    logits = dot(w_out[...], line3[...].reshape(hidden, nodes))
    rows = lax.broadcasted_iota(jnp.int32, logits.shape, 0)
    real = rows < classes
    log_total = jnp.log(jnp.sum(jnp.where(real, jnp.exp(logits), 0.0), axis=0, keepdims=True))
    one_hot = jnp.where(rows == labels[...], 1.0, 0.0)
    picked = jnp.sum(one_hot * logits, axis=0, keepdims=True)
    weighting = mask[...].astype(F32)
    loss_part = jnp.sum(weighting * (log_total - picked))
    count_part = jnp.sum(weighting)
    grads = jnp.where(real, weighting * (jnp.exp(logits - log_total) - one_hot), 0.0).astype(BF16)
    third = dot(out_rows[...], grads).astype(BF16)
    for rb in range(rb_count):
        back[rb] = third[:, lanes(rb)]
    hp = line3.shape[1]
    go_mine[...] = jnp.zeros_like(go_mine)
    go_mine[0:hp, 0 : grads.shape[0]] = dot_nt(line3[f], grads)
    stat_rows = lax.broadcasted_iota(jnp.int32, (8, go_mine.shape[1]), 0)
    go_mine[hp : hp + 8, :] = jnp.where(stat_rows == 0, loss_part, count_part)
    go_sum = Total(0, go_mine, go_part, go_pair, go_recv)
    go_sum.near().start()

    spread(0, acc)
    go_sum.spread_pair()
    for rb in range(rb_count):
        line4[f, :, lanes(rb)] = (acc[rb] * elu_slope(pre2[:, lanes(rb)])).astype(BF16)
    gather = Line(line4, line_sems.at[3], nf)
    gather.start()
    gather.finish()
    gate = line4[...].reshape(hidden, nodes)
    second = dot(mid_rows[...], gate).astype(BF16)
    for rb in range(rb_count):
        back[rb] = second[:, lanes(rb)]
    gm_mine[...] = dot_nt(line2[f], gate)
    gm_sum = Total(1, gm_mine, gm_part, gm_pair, gm_recv)
    gm_sum.near().start()

    spread(1, acc)
    gm_sum.spread_pair()
    for rb in range(rb_count):
        line5[f, :, lanes(rb)] = (acc[rb] * elu_slope(pre1[:, lanes(rb)])).astype(BF16)
    gather = Line(line5, line_sems.at[4], nf)
    gather.start()
    gather.finish()
    gate = line5[...].reshape(hidden, nodes)
    gi_mine[...] = dot_nt(line1[f], gate)
    gi_sum = Total(2, gi_mine, gi_part, gi_pair, gi_recv)
    gi_sum.near().start()
    gi_sum.spread_pair()
    total = go_sum.result()
    gout_out[...] = total[0:hp, 0:classes]
    loss_out[...] = total[hp : hp + 1, 0:1] / jnp.maximum(total[hp + 1 : hp + 2, 0:1], 1.0)
    gmid_out[...] = gm_sum.result()
    gin_out[...] = gi_sum.result()


def round_up(value, step):
    return (value + step - 1) // step * step


def shards(
    features, weight_in, weight_mid, weight_out, block_values,
    block_dst, block_src, block_count, labels, train_mask,
):
    n = lax.axis_size("blk")
    nf = lax.axis_size("feat")
    f = lax.axis_index("feat")
    in_part, nodes = features.shape
    hidden, classes = weight_out.shape
    hp = hidden // nf
    slots, blk = block_values.shape[2], block_values.shape[-1]
    rb_count = nodes // blk
    padded = round_up(classes, 16)
    wide = round_up(classes, 128)
    chips = n // 2

    w_in = lax.dynamic_slice_in_dim(weight_in, f * hp, hp, 1).T
    w_in = w_in.reshape(hp, nf, in_part).transpose(1, 0, 2)
    w_mid = lax.dynamic_slice_in_dim(weight_mid, f * hp, hp, 1).T
    out_pad = jnp.pad(weight_out, ((0, 0), (0, padded - classes)))
    w_out = out_pad.T
    out_rows = lax.dynamic_slice_in_dim(out_pad, f * hp, hp, 0)
    mid_rows = lax.dynamic_slice_in_dim(weight_mid, f * hp, hp, 0)
    live = jnp.arange(slots, dtype=jnp.int32)[None, :] < block_count[0][:, None]
    blocks = jnp.arange(rb_count, dtype=jnp.int32)
    w_fwd = ((block_dst[0][:, :, None] == blocks) & live[:, :, None]).astype(F32).reshape(-1)
    w_bwd = ((block_src[0][:, :, None] == blocks) & live[:, :, None]).astype(F32).reshape(-1)

    vmem = pl.BlockSpec(memory_space=pltpu.VMEM)
    smem = pl.BlockSpec(memory_space=pltpu.SMEM)

    def sums(rows, width):
        return [pltpu.VMEM((rows, width), F32)] * 3 + [pltpu.VMEM((chips, rows, width), F32)]

    tab = pltpu.VMEM((n, rb_count, hp, blk), BF16)
    line = pltpu.VMEM((nf, hp, nodes), BF16)
    stage = pltpu.VMEM((2, chips, rb_count, hp, blk), BF16)
    loss, gin, gmid, gout = pl.pallas_call(
        functools.partial(step_kernel, n, nf, classes, slots),
        out_shape=(
            jax.ShapeDtypeStruct((1, 1), F32),
            jax.ShapeDtypeStruct((in_part, hidden), F32),
            jax.ShapeDtypeStruct((hp, hidden), F32),
            jax.ShapeDtypeStruct((hp, classes), F32),
        ),
        in_specs=[vmem] * 7 + [smem] * 4 + [vmem] * 2,
        out_specs=(vmem,) * 4,
        scratch_shapes=[
            pltpu.VMEM((n, rb_count, in_part, blk), BF16), tab, tab,
            pltpu.VMEM((nf, in_part, nodes), BF16), line, line, line, line,
            pltpu.VMEM((rb_count, hp, blk), BF16),
            pltpu.VMEM((rb_count, hp, blk), F32),
            pltpu.VMEM((slots, hp, blk), F32),
            pltpu.VMEM((rb_count, in_part, blk), BF16),
            pltpu.VMEM((rb_count, in_part, blk), F32),
            pltpu.VMEM((slots, in_part, blk), F32),
            pltpu.VMEM((hp, nodes), F32), pltpu.VMEM((hp, nodes), F32),
            stage, stage, stage, stage,
            *sums(hp + 8, wide), *sums(hp, hidden), *sums(in_part, hidden),
            pltpu.SemaphoreType.DMA((3, 4, chips)),
            pltpu.SemaphoreType.DMA((5, 4, nf + 1)),
            pltpu.SemaphoreType.DMA((2, 4, chips)),
            pltpu.SemaphoreType.DMA((3, 2, chips)),
        ],
        compiler_params=pltpu.CompilerParams(
            collective_id=0, has_side_effects=True, vmem_limit_bytes=56 * 1024 * 1024
        ),
        name="step",
    )(
        features, w_in, w_mid, w_out, out_rows, mid_rows, block_values[0],
        block_dst.reshape(-1), block_src.reshape(-1), w_fwd, w_bwd,
        labels.reshape(1, -1), train_mask.reshape(1, -1),
    )
    return loss.reshape(()), gin, gmid, gout


def solution(mesh):
    placed = (
        P("feat", "blk"), P(), P(), P(), P("blk", None, None, None, None),
        P("blk", None, None), P("blk", None, None), P("blk", None), P("blk"), P("blk"),
    )
    return jax.shard_map(
        shards,
        mesh=mesh,
        in_specs=placed,
        out_specs=(P(), P("feat", None), P("feat", None), P("feat", None)),
        check_vma=False,
    )
```

time: 615 us -> 145 us (0.24)
  other arithmetic: 142 us -> 1.54 us
  waiting for transfers between devices: 134 us -> 0 us
  Pallas kernels: 0 us -> 127 us
  blocking collectives: 113 us -> 0 us
  local copies, waits for them, and re-layouts: 106 us -> 13.7 us
  matrix products: 63.7 us -> 0 us
  loops' own time: 33.6 us -> 0 us
  between operations: 16.4 us -> 2.43 us
    pallas_call x0 -> x1, Pallas kernels: none -> 127 us  [shards(): pl.pallas_call(functools.partial(step_kernel, n, nf, classes, slots), out...]
    all_gather x6 -> x0, blocking collectives: 88.5 us -> none  [the longest x2 30.8 us: weight_columns(): lax.all_gather(gated, 'feat', axis=0, tiled=True)]
    reduce_scatter x2 -> x0, waiting for transfers between devices: 71 us -> none  [spread_back(): lax.psum_scatter(lax.map(term_one_panel, jnp.arange(lax.axis_size('blk')...]
    dot_general x48 -> x0, matrix products: 63.7 us -> none  [the longest x24 36.4 us: folding_one_panel(): jnp.einsum('fsj,sij->fsi', chosen, values[0, turn_index], preferred_eleme...]
    dynamic_slice x56 -> x4, local copies, waits for them, and re-layouts: 59 us -> 2.16 us  [the longest x1 0.83 us: shards(): w_in = lax.dynamic_slice_in_dim(weight_in, f * hp, hp, 1).T]
    scatter-add x40 -> x0, other arithmetic: 53.7 us -> none  [the longest x24 31.2 us: folding_one_panel(): accumulated.at[:, targets[0, turn_index]]]
    all_gather x2 -> x0, waiting for transfers between devices: 48.1 us -> none  [hidden_aggregate(): lax.all_gather(table, 'blk', axis=1, tiled=True)]
    and x32 -> x0, other arithmetic: 43 us -> none  [the longest x16 21.5 us: folding_one_panel(): chosen = jnp.take(window, sources[0, turn_index], axis=1)]
  transfers between devices with their start and end apart: 5 -> 0, of which waited for: 5 -> 0; matrix products, arithmetic and copies ran while one was open for 1% -> 0% of each run, Pallas kernels for 0% -> 0%
where the time goes in v1:
time: 145 us; the launch traced here: 144 us
  Pallas kernels  127 us (88%)
  local copies, waits for them, and re-layouts  13.7 us (9%)
  between operations  2.43 us (2%)
  other arithmetic  1.54 us (1%)
    pallas_call x1, Pallas kernels, shards(): pl.pallas_call(functools.partial(step_kernel, n, nf, classes, slots), out...  127 us
    unnamed x7, local copies, waits for them, and re-layouts  6.06 us

profile of v1, /device:TPU:0, one launch (start us, length us, event | category | flops | bytes accessed | tf_op | source)
XLA Modules:
  0.0 144.2 jit_solution(3350582736287890707)
XLA Ops:
  0.6 0.0 copy-start
  0.7 1.0 copy.19
  1.7 0.6 pad_dynamic-slice_fusion.out_rows
  2.3 0.8 constant_dynamic-slice_fusion.2
  3.1 0.7 copy.17
  3.9 0.0 copy-done
  3.9 0.1 constant_dynamic-slice_fusion.1
  4.0 0.7 copy.21
  4.7 0.6 constant_dynamic-slice_fusion.mid_rows
  5.3 0.7 copy.20.w_out
  6.1 0.7 iota_compare_fusion.2
  6.8 0.8 fusion.3
  7.6 0.7 reshape.74.w_fwd
  8.3 0.7 reshape.75.w_bwd
  9.0 1.3 reshape.69.dst
  10.2 1.3 reshape.70.src
  11.6 126.6 %step.1 = (f32[1,1]{1,0:T(1,128)}, f32[32,256]{1,0:T(8,128)}, f32[64,256]{1,0:T(8,128)}, f32[64,172]{1,0:T(8,128)}) custom-call(bf16[32,1024]{1,0:T(8,128)(2,1)} %features.1, bf16[4,64,32]{2,1,0:T(8,128)(2,1)} %bitcast.15, bf16[64,256]{1,0:T(8,128)(2,1)} %bitcast.16, bf16[176,256]{1,0:T(8,128)(2,1)} %copy.20.w_out, ...), custom_call_target="tpu_custom_call" | custom-call | tf_op jit(solution)/shard_map/step/pallas_call | solution.py:402
  138.8 1.4 copy.27
  140.1 1.5 %copy.28 = f32[64,256]{1,0:T(8,128)} copy(f32[64,256]{1,0:T(8,128)} %get-tuple-element.20) | data formatting | bytes 131072
  141.6 1.5 %copy.29 = f32[64,172]{1,0:T(8,128)} copy(f32[64,172]{1,0:T(8,128)} %get-tuple-element.21) | data formatting | bytes 88064
  (1 shorter events, 0.0 us)
Async XLA Ops:
  0.6 3.2 %copy-start = (bf16[256,256]{1,0:T(8,128)(2,1)S(1)}, bf16[256,256]{1,0:T(8,128)(2,1)}, u32[]{:S(2)}) copy-start(bf16[256,256]{1,0:T(8,128)(2,1)} %param.12) | copy-start | bytes 393220

commit v2 on v1

v2 whole, which is shorter than its diff:
```python
import functools

import jax
import jax.numpy as jnp
from jax import lax
from jax.experimental import pallas as pl
from jax.experimental.pallas import tpu as pltpu
from jax.sharding import PartitionSpec as P

MESH = pl.DeviceIdType.MESH
NT = (((1,), (1,)), ((), ()))
F32 = jnp.float32
BF16 = jnp.bfloat16


def dot(a, b):
    return jnp.dot(a, b, preferred_element_type=F32)


def dot_nt(a, b):
    return lax.dot_general(a, b, NT, preferred_element_type=F32)


def elu(v):
    return jnp.where(v > 0, v, jnp.exp(jnp.minimum(v, 0.0)) - 1.0)


def elu_slope(v):
    return jnp.where(v > 0, 1.0, jnp.exp(jnp.minimum(v, 0.0)))


class Line:
    def __init__(self, table, sems, nf):
        self.table, self.sems, self.nf = table, sems, nf
        self.f = lax.axis_index("feat")

    def right(self, k):
        return pltpu.make_async_remote_copy(
            src_ref=self.table.at[self.f - k],
            dst_ref=self.table.at[self.f - k],
            send_sem=self.sems.at[0, k],
            recv_sem=self.sems.at[1, k + 1],
            device_id={"feat": self.f + 1},
            device_id_type=MESH,
        )

    def left(self, k):
        return pltpu.make_async_remote_copy(
            src_ref=self.table.at[self.f + k],
            dst_ref=self.table.at[self.f + k],
            send_sem=self.sems.at[2, k],
            recv_sem=self.sems.at[3, k + 1],
            device_id={"feat": self.f - 1},
            device_id_type=MESH,
        )

    def arrived(self, sem, slot):
        pltpu.make_async_copy(self.table.at[slot], self.table.at[slot], sem).wait()

    def start(self):
        @pl.when(self.f < self.nf - 1)
        def _():
            self.right(0).start()

        @pl.when(self.f > 0)
        def _():
            self.left(0).start()

    def finish(self):
        f, nf = self.f, self.nf
        for k in range(1, nf):

            @pl.when(f >= k)
            def _():
                self.arrived(self.sems.at[1, k], f - k)

                @pl.when(f < nf - 1)
                def _():
                    self.right(k).start()

            @pl.when(f + k <= nf - 1)
            def _():
                self.arrived(self.sems.at[3, k], f + k)

                @pl.when(f > 0)
                def _():
                    self.left(k).start()

    def drain(self):
        f, nf = self.f, self.nf
        for k in range(nf):

            @pl.when(jnp.logical_and(f >= k, f < nf - 1))
            def _():
                self.right(k).wait_send()

            @pl.when(jnp.logical_and(f + k <= nf - 1, f > 0))
            def _():
                self.left(k).wait_send()


def step_kernel(
    n, nf, chunks, slots,
    features, w_in, w_mid, w_out, values, dst, src, count, labels, mask,
    loss_out, gin_out, gmid_out, gout_out,
    tab1, tab2, tab3, line1, line2, line3, line4,
    back, acc, prod, win1, acc1, prod1, pre1, pre2, w_in_t, w_mid_t, gate1,
    out_p, recv_p, out_s, recv_s,
    go_mine, go_part, go_pair, go_recv,
    gm_mine, gm_part, gm_pair, gm_recv,
    gi_mine, gi_part, gi_pair, gi_recv, gi_own, gi_swap,
    blk_sems, line_sems, rs_sems, sum_sems, swap_sems,
):
    me = lax.axis_index("blk")
    f = lax.axis_index("feat")
    chip = me // 2
    side = me % 2
    chips = n // 2
    partner = chip * 2 + (1 - side)
    rb_count = tab2.shape[1]
    blk = tab2.shape[3]
    in_part = features.shape[0]
    hp = tab2.shape[2]
    hidden = nf * hp
    part = rb_count // chunks
    classes = w_out.shape[1]

    def far(k):
        return lax.rem(chip + k, chips) * 2 + side

    barrier = pltpu.get_barrier_semaphore()
    pl.semaphore_signal(barrier, inc=1, device_id={"blk": partner}, device_id_type=MESH)
    for k in range(1, chips):
        pl.semaphore_signal(barrier, inc=1, device_id={"blk": far(k)}, device_id_type=MESH)
    for k in range(1, nf):
        pl.semaphore_signal(
            barrier, inc=1, device_id={"feat": lax.rem(f + k, nf)}, device_id_type=MESH
        )
    pl.semaphore_wait(barrier, chips + nf - 1)

    def remote(source, target, send, recv, device):
        return pltpu.make_async_remote_copy(
            src_ref=source, dst_ref=target, send_sem=send, recv_sem=recv,
            device_id={"blk": device}, device_id_type=MESH,
        )

    def lanes(rb):
        return slice(rb * blk, (rb + 1) * blk)

    def own_rows(ref):
        return ref[pl.ds(pl.multiple_of(f * hp, hp), hp), :]

    def combined(product, target, index, panel, add):
        live = count[0, panel]
        places = [jnp.where(s < live, index[0, panel, s], -1) for s in range(slots)]
        for rb in range(rb_count):
            total = target[rb] if add else None
            for s in range(slots):
                term = product[s] * jnp.where(places[s] == rb, 1.0, 0.0)
                total = term if total is None else total + term
            target[rb] = total

    def piece(table, panel, c):
        return table.at[panel, pl.ds(c * part, part)]

    class Gather:
        def __init__(self, table, phase):
            self.table, self.phase = table, phase

        def to_far(self, k, c):
            return remote(piece(self.table, me, c), piece(self.table, me, c),
                          blk_sems.at[self.phase, 0, k, c],
                          blk_sems.at[self.phase, 1, k, c], far(k))

        def to_partner(self, k, c):
            panel = lax.rem(chip - k + chips, chips) * 2 + side
            return remote(piece(self.table, panel, c), piece(self.table, panel, c),
                          blk_sems.at[self.phase, 2, k, c],
                          blk_sems.at[self.phase, 3, k, c], partner)

        def start(self, c):
            for k in range(1, chips):
                self.to_far(k, c).start()
            self.to_partner(0, c).start()

        def aggregate(self, total, product, window):
            total[...] = jnp.zeros_like(total)

            def turn(t, carry):
                k = t // 2
                h = t % 2
                base = lax.rem(chip - k + chips, chips) * 2

                @pl.when(jnp.logical_and(h == 0, k > 0))
                def _():
                    for c in range(chunks):
                        self.to_far(k, c).wait_recv()
                        self.to_partner(k, c).start()

                @pl.when(h == 1)
                def _():
                    for c in range(chunks):
                        self.to_partner(k, c).wait_recv()

                panel = base + jnp.where(h == 0, side, 1 - side)
                window[...] = self.table[panel]
                for s in range(slots):
                    chosen = window[src[0, panel, s]]
                    product[s] = dot_nt(chosen, values[0, panel, s])
                combined(product, total, dst, panel, True)
                return carry

            lax.fori_loop(0, n, turn, 0)
            for c in range(chunks):
                for k in range(1, chips):
                    self.to_far(k, c).wait_send()
                for k in range(chips):
                    self.to_partner(k, c).wait_send()

    def spread(phase, own, ready):
        def to_partner(k):
            return remote(out_p.at[phase, k], recv_p.at[phase, k], rs_sems.at[phase, 0, k, 0],
                          rs_sems.at[phase, 1, k, 0], partner)

        def to_far(k, c):
            rows = pl.ds(c * part, part)
            return remote(out_s.at[phase, k, rows], recv_s.at[phase, k, rows],
                          rs_sems.at[phase, 2, k, c], rs_sems.at[phase, 3, k, c], far(k))

        def turn(t, carry):
            k = lax.rem(t // 2 + 1, chips)
            h = t % 2
            panel = lax.rem(chip + k, chips) * 2 + jnp.where(h == 0, 1 - side, side)
            for s in range(slots):
                chosen = back[dst[0, panel, s]]
                prod[s] = dot(chosen, values[0, panel, s])
            combined(prod, own, src, panel, False)

            @pl.when(h == 0)
            def _():
                out_p[phase, k] = own[...].astype(BF16)
                to_partner(k).start()

            @pl.when(h == 1)
            def _():
                to_partner(k).wait_recv()
                own[...] += recv_p[phase, k].astype(F32)

                @pl.when(k > 0)
                def _():
                    out_s[phase, k] = own[...].astype(BF16)
                    to_far(k, 0).start()

            return carry

        lax.fori_loop(0, n, turn, 0)
        for c in range(1, chunks):
            for k in range(1, chips):
                to_far(k, c).start()
        for c in range(chunks):
            for k in range(1, chips):
                to_far(k, c).wait_recv()
            for rb in range(c * part, (c + 1) * part):
                total = own[rb]
                for k in range(1, chips):
                    total = total + recv_s[phase, k, rb].astype(F32)
                ready(c, rb, total)
            ready(c, None, None)
        for c in range(chunks):
            for k in range(1, chips):
                to_far(k, c).wait_send()
        for k in range(chips):
            to_partner(k).wait_send()

    class Total:
        def __init__(self, index, mine, part, pair, recv):
            self.index, self.mine, self.part, self.pair, self.recv = index, mine, part, pair, recv

        def near(self):
            return remote(self.mine, self.part, sum_sems.at[self.index, 0, 0],
                          sum_sems.at[self.index, 1, 0], partner)

        def wide(self, k):
            return remote(self.pair, self.recv.at[chip], sum_sems.at[self.index, 0, k],
                          sum_sems.at[self.index, 1, k], far(k))

        def spread_pair(self):
            self.near().wait_recv()
            self.pair[...] = self.mine[...] + self.part[...]
            for k in range(1, chips):
                self.wide(k).start()

        def result(self):
            self.recv[chip] = self.pair[...]
            for k in range(1, chips):
                source = lax.rem(chip - k + chips, chips)
                remote(self.pair, self.recv.at[source], sum_sems.at[self.index, 0, k],
                       sum_sems.at[self.index, 1, k], far(k)).wait_recv()
            total = self.recv[0]
            for c in range(1, chips):
                total = total + self.recv[c]
            self.near().wait_send()
            for k in range(1, chips):
                self.wide(k).wait_send()
            return total

    def lines(table, phase):
        return [Line(table.at[c], line_sems.at[phase, c], nf) for c in range(chunks)]

    def gather_total(total, table, phase):
        gathers = lines(table, phase)
        for c in range(chunks):
            for i in range(part):
                table[c, f, :, lanes(i)] = total[c * part + i].astype(BF16)
            gathers[c].start()
        return gathers

    def place(target, value, c):
        for i in range(part):
            target[me, c * part + i] = value[:, lanes(i)]

    first = Gather(tab1, 0)
    for c in range(chunks):
        for rb in range(c * part, (c + 1) * part):
            tab1[me, rb] = features[:, lanes(rb)]
        first.start(c)
    w_in_t[...] = w_in[...].T
    w_mid_t[...] = w_mid[...].T
    first.aggregate(acc1, prod1, win1)
    gathers = gather_total(acc1, line1, 0)
    follow = Gather(tab2, 1)
    own_in = own_rows(w_in_t)
    for c in range(chunks):
        gathers[c].finish()
        if in_part % 16 == 0:
            pre = dot(own_in, line1[c].reshape(nf * in_part, part * blk))
        else:
            pre = dot(own_in[:, 0:in_part], line1[c, 0])
            for g in range(1, nf):
                pre += dot(own_in[:, g * in_part : (g + 1) * in_part], line1[c, g])
        pre1[c] = pre
        place(tab2, elu(pre).astype(BF16), c)
        follow.start(c)
    for g in gathers:
        g.drain()

    follow.aggregate(acc, prod, back)
    gathers = gather_total(acc, line2, 1)
    follow = Gather(tab3, 2)
    for c in range(chunks):
        gathers[c].finish()
        pre = dot(own_rows(w_mid_t), line2[c].reshape(hidden, part * blk))
        pre2[c] = pre
        place(tab3, elu(pre).astype(BF16), c)
        follow.start(c)
    for g in gathers:
        g.drain()

    follow.aggregate(acc, prod, back)
    gathers = gather_total(acc, line3, 2)
    loss_part = 0.0
    count_part = 0.0
    grad_part = None
    for c in range(chunks):
        gathers[c].finish()
        span = slice(c * part * blk, (c + 1) * part * blk)
        logits = lax.dot_general(
            w_out[...], line3[c].reshape(hidden, part * blk), (((0,), (0,)), ((), ())),
            preferred_element_type=F32,
        )
        rows = lax.broadcasted_iota(jnp.int32, logits.shape, 0)
        log_total = jnp.log(jnp.sum(jnp.exp(logits), axis=0, keepdims=True))
        one_hot = jnp.where(rows == labels[:, span], 1.0, 0.0)
        picked = jnp.sum(one_hot * logits, axis=0, keepdims=True)
        weighting = mask[:, span].astype(F32)
        loss_part += jnp.sum(weighting * (log_total - picked))
        count_part += jnp.sum(weighting)
        grads = (weighting * (jnp.exp(logits - log_total) - one_hot)).astype(BF16)
        third = dot(own_rows(w_out), grads).astype(BF16)
        for i in range(part):
            back[c * part + i] = third[:, lanes(i)]
        term = dot_nt(line3[c, f], grads)
        grad_part = term if grad_part is None else grad_part + term
    for g in gathers:
        g.drain()
    go_mine[...] = jnp.zeros_like(go_mine)
    go_mine[0:hp, 0:classes] = grad_part
    stat_rows = lax.broadcasted_iota(jnp.int32, (8, go_mine.shape[1]), 0)
    go_mine[hp : hp + 8, :] = jnp.where(stat_rows == 0, loss_part, count_part)
    go_sum = Total(0, go_mine, go_part, go_pair, go_recv)
    go_sum.near().start()

    gathers = lines(line4, 3)

    def ready_second(c, rb, total):
        if rb is None:
            gathers[c].start()
        else:
            i = rb - c * part
            slope = elu_slope(pre2[c, :, lanes(i)])
            line4[c, f, :, lanes(i)] = (total * slope).astype(BF16)

    spread(0, acc, ready_second)
    go_sum.spread_pair()
    grad_part = None
    for c in range(chunks):
        gathers[c].finish()
        gate = line4[c].reshape(hidden, part * blk)
        second = dot(own_rows(w_mid), gate).astype(BF16)
        for i in range(part):
            back[c * part + i] = second[:, lanes(i)]
        term = dot_nt(line2[c, f], gate)
        grad_part = term if grad_part is None else grad_part + term
    for g in gathers:
        g.drain()
    gm_mine[...] = grad_part
    gm_sum = Total(1, gm_mine, gm_part, gm_pair, gm_recv)
    gm_sum.near().start()

    def ready_first(c, rb, total):
        if rb is not None:
            i = rb - c * part
            slope = elu_slope(pre1[c, :, lanes(i)])
            gate1[c, :, lanes(i)] = (total * slope).astype(BF16)

    spread(1, acc, ready_first)
    gm_sum.spread_pair()
    for g in range(nf):
        term = dot_nt(line1[0, g], gate1[0])
        for c in range(1, chunks):
            term += dot_nt(line1[c, g], gate1[c])
        gi_own[g] = term

    def swap(k):
        target = lax.rem(f + k, nf)
        return pltpu.make_async_remote_copy(
            src_ref=gi_own.at[target], dst_ref=gi_swap.at[f],
            send_sem=swap_sems.at[0, k], recv_sem=swap_sems.at[1, k],
            device_id={"feat": target}, device_id_type=MESH,
        )

    for k in range(1, nf):
        swap(k).start()
    gi_swap[f] = gi_own[f]
    total = go_sum.result()
    gout_out[...] = total[0:hp, 0:classes]
    loss_out[...] = total[hp : hp + 1, 0:1] / jnp.maximum(total[hp + 1 : hp + 2, 0:1], 1.0)
    gmid_out[...] = gm_sum.result()
    for k in range(1, nf):
        slot = gi_swap.at[lax.rem(f - k + nf, nf)]
        pltpu.make_async_copy(slot, slot, swap_sems.at[1, k]).wait()
    for g in range(nf):
        gi_mine[:, g * hp : (g + 1) * hp] = gi_swap[g]
    gi_sum = Total(2, gi_mine, gi_part, gi_pair, gi_recv)
    gi_sum.near().start()
    gi_sum.spread_pair()
    for k in range(1, nf):
        swap(k).wait_send()
    gin_out[...] = gi_sum.result()


def round_up(value, step):
    return (value + step - 1) // step * step


def shards(
    features, weight_in, weight_mid, weight_out, block_values,
    block_dst, block_src, block_count, labels, train_mask,
):
    n = lax.axis_size("blk")
    nf = lax.axis_size("feat")
    in_part, nodes = features.shape
    hidden, classes = weight_out.shape
    hp = hidden // nf
    slots, blk = block_values.shape[2], block_values.shape[-1]
    rb_count = nodes // blk
    wide = round_up(classes, 128)
    chips = n // 2
    chunks = 2 if rb_count % 2 == 0 else 1
    span = nodes // chunks

    vmem = pl.BlockSpec(memory_space=pltpu.VMEM)
    smem = pl.BlockSpec(memory_space=pltpu.SMEM)

    def sums(rows, width):
        return [pltpu.VMEM((rows, width), F32)] * 3 + [pltpu.VMEM((chips, rows, width), F32)]

    tab = pltpu.VMEM((n, rb_count, hp, blk), BF16)
    line = pltpu.VMEM((chunks, nf, hp, span), BF16)
    stage = pltpu.VMEM((2, chips, rb_count, hp, blk), BF16)
    loss, gin, gmid, gout = pl.pallas_call(
        functools.partial(step_kernel, n, nf, chunks, slots),
        out_shape=(
            jax.ShapeDtypeStruct((1, 1), F32),
            jax.ShapeDtypeStruct((in_part, hidden), F32),
            jax.ShapeDtypeStruct((hp, hidden), F32),
            jax.ShapeDtypeStruct((hp, classes), F32),
        ),
        in_specs=[vmem] * 5 + [smem] * 3 + [vmem] * 2,
        out_specs=(vmem,) * 4,
        scratch_shapes=[
            pltpu.VMEM((n, rb_count, in_part, blk), BF16), tab, tab,
            pltpu.VMEM((chunks, nf, in_part, span), BF16), line, line, line,
            pltpu.VMEM((rb_count, hp, blk), BF16),
            pltpu.VMEM((rb_count, hp, blk), F32),
            pltpu.VMEM((slots, hp, blk), F32),
            pltpu.VMEM((rb_count, in_part, blk), BF16),
            pltpu.VMEM((rb_count, in_part, blk), F32),
            pltpu.VMEM((slots, in_part, blk), F32),
            pltpu.VMEM((chunks, hp, span), F32), pltpu.VMEM((chunks, hp, span), F32),
            pltpu.VMEM((hidden, weight_in.shape[0]), BF16),
            pltpu.VMEM((hidden, hidden), BF16),
            pltpu.VMEM((chunks, hp, span), BF16),
            stage, stage, stage, stage,
            *sums(hp + 8, wide), *sums(hp, hidden), *sums(in_part, hidden),
            pltpu.VMEM((nf, in_part, hp), F32), pltpu.VMEM((nf, in_part, hp), F32),
            pltpu.SemaphoreType.DMA((3, 4, chips, chunks)),
            pltpu.SemaphoreType.DMA((4, chunks, 4, nf + 1)),
            pltpu.SemaphoreType.DMA((2, 4, chips, chunks)),
            pltpu.SemaphoreType.DMA((3, 2, chips)),
            pltpu.SemaphoreType.DMA((2, nf)),
        ],
        compiler_params=pltpu.CompilerParams(
            collective_id=0, has_side_effects=True, vmem_limit_bytes=56 * 1024 * 1024
        ),
        name="step",
    )(
        features, weight_in, weight_mid, weight_out, block_values,
        block_dst, block_src, block_count, labels.reshape(1, -1), train_mask.reshape(1, -1),
    )
    return loss.reshape(()), gin, gmid, gout


def solution(mesh):
    placed = (
        P("feat", "blk"), P(), P(), P(), P("blk", None, None, None, None),
        P("blk", None, None), P("blk", None, None), P("blk", None), P("blk"), P("blk"),
    )
    return jax.shard_map(
        shards,
        mesh=mesh,
        in_specs=placed,
        out_specs=(P(), P("feat", None), P("feat", None), P("feat", None)),
        check_vma=False,
    )
```

time: 145 us -> 128 us (0.88)
  Pallas kernels: 127 us -> 119 us
  local copies, waits for them, and re-layouts: 13.7 us -> 5.97 us
  other arithmetic: 1.54 us -> 0 us
    pallas_call x1, Pallas kernels: 127 us -> 119 us  [shards(): pl.pallas_call(functools.partial(step_kernel, n, nf, chunks, slots), out_...]
    reshape x3 -> x0, local copies, waits for them, and re-layouts: 3.32 us -> none  [the longest x1 1.31 us: shards(): block_src.reshape(-1)]
    dynamic_slice x4 -> x0, local copies, waits for them, and re-layouts: 2.16 us -> none  [the longest x1 0.83 us: shards(): w_in = lax.dynamic_slice_in_dim(weight_in, f * hp, hp, 1).T]
    unnamed x7 -> x4, local copies, waits for them, and re-layouts: 6.06 us -> 5.97 us
where the time goes in v2:
time: 128 us; the launch traced here: 127 us
  Pallas kernels  119 us (93%)
  local copies, waits for them, and re-layouts  5.97 us (5%)
  between operations  2.45 us (2%)
    pallas_call x1, Pallas kernels, shards(): pl.pallas_call(functools.partial(step_kernel, n, nf, chunks, slots), out_...  119 us
    unnamed x4, local copies, waits for them, and re-layouts  5.97 us

profile of v2, /device:TPU:0, one launch (start us, length us, event | category | flops | bytes accessed | tf_op | source)
XLA Modules:
  0.0 127.2 jit_solution(13930525658916404548)
XLA Ops:
  0.6 1.6 %copy.14.w_out = bf16[256,172]{1,0:T(8,128)(2,1)} copy(bf16[256,172]{0,1:T(8,128)(2,1)} %param.13) | data formatting | bytes 176128 | tf_op args[3]
  2.3 118.8 %step.1 = (f32[1,1]{1,0:T(1,128)}, f32[32,256]{1,0:T(8,128)}, f32[64,256]{1,0:T(8,128)}, f32[64,172]{1,0:T(8,128)}) custom-call(bf16[32,1024]{1,0:T(8,128)(2,1)} %features.1, bf16[128,256]{1,0:T(8,128)(2,1)} %w_in.1, bf16[256,256]{1,0:T(8,128)(2,1)} %w_mid.1, bf16[256,172]{1,0:T(8,128)(2,1)} %copy.14.w_out, bf16[1,8,16,128,128]{4,3,2,1,0:T(8,128)(2,1)} %values.1, ...), custom_call_target="tpu_custom_call" | custom-call | tf_op jit(solution)/shard_map/step/pallas_call | solution.py:491
  121.8 1.4 %copy.20 = f32[32,256]{1,0:T(8,128)} copy(f32[32,256]{1,0:T(8,128)} %get-tuple-element.17) | data formatting | bytes 65536
  123.1 1.5 %copy.21 = f32[64,256]{1,0:T(8,128)} copy(f32[64,256]{1,0:T(8,128)} %get-tuple-element.18) | data formatting | bytes 131072
  124.6 1.5 %copy.22 = f32[64,172]{1,0:T(8,128)} copy(f32[64,172]{1,0:T(8,128)} %get-tuple-element.19) | data formatting | bytes 88064
